TPU v7x, 256 devices: a whole 4x4x8 slice. The times are simulated.
256 devices in a mesh: grp: 8 (over y, core), dev: 32 (over z, x).
Axes of the slice: x: 4, y: 4, z: 8, core: 2. Of those that a mesh axis runs over, the one named last changes fastest.
Arguments:
- a_blocks: bfloat16 [8192, 7, 128, 128], P(('grp', 'dev')), may hold values from -0.5 to 0.5
- p_blocks: bfloat16 [8192, 128, 128], P(('grp', 'dev')), may hold values from -0.5 to 0.5
- neighbours: int32 [8192, 6], P(('grp', 'dev')), may hold values from 0 to 31
- coarse_slot: int32 [8192, 7], P(('grp', 'dev')), may hold values from 0 to 6
- owner: int32 [8192, 1], P(('grp', 'dev')), may hold values from 0 to 31; in each aligned block of 32 rows (0 to 31, 32 to 63, ...) at most 2 rows name the same one
- agg_local: int32 [8192], P(('grp', 'dev')), may hold values from 0 to 7
Outputs:
- coarse: bfloat16 [2048, 7, 128, 128], P(('grp', 'dev'))
Inputs may be any that keep to these rules, and one draw needn't show every extreme that they name: Among the elements of one device at most 2 have the same owner, and in every draw some device has exactly 2 elements with one owner.
All inputs are finite; a program needn't handle non-finite values.
Results may differ from a plain program's by a relative error of at most 0.008.
Values may be sent and summed in bfloat16 or wider, within the bound.
A program may use at most 128 MiB of HBM per device.

v0:
```python
import jax
import jax.numpy as jnp
from jax import lax
from jax.sharding import PartitionSpec as P

KC = 7


def with_halo(block, sides, width):
    for axis, dim in sides:
        count = lax.axis_size(axis)
        forward = [(i, i + 1) for i in range(count - 1)]
        backward = [(target, source) for source, target in forward]
        low = lax.ppermute(
            lax.slice_in_dim(block, block.shape[dim] - width, None, axis=dim), axis, forward
        )
        high = lax.ppermute(lax.slice_in_dim(block, 0, width, axis=dim), axis, backward)
        block = jnp.concatenate([low, block, high], axis=dim)
    return block


def slot_table(slot_rows):
    return (slot_rows[:, :, None] == jnp.arange(KC, dtype=jnp.int32)[None, None, :]).astype(
        jnp.float32
    )


def on_device(a_blocks, p_blocks, neighbours, coarse_slot, owner, agg_local):
    elems = p_blocks.shape[0]
    width = p_blocks.shape[1]
    groups = lax.axis_size("dev")
    cap = max(2, 2 * elems // groups)
    rows = groups * cap
    aggs = elems // 4
    lifted = p_blocks.reshape(1, 1, elems, width, width)
    padded = with_halo(lifted, (("grp", 0), ("dev", 1)), 1)
    sources = (
        p_blocks,
        p_blocks,
        padded[1, 0, :],
        padded[1, 2, :],
        padded[0, 1, :],
        padded[2, 1, :],
    )
    faces = [p_blocks] + [jnp.take(sources[face], neighbours[:, face], axis=0) for face in range(6)]
    facing = jnp.stack(faces, 1)
    applied = jnp.einsum(
        "efik,efkj->efij", a_blocks, facing, preferred_element_type=jnp.float32
    ).astype(jnp.bfloat16)
    targets = owner[:, 0]
    order = jnp.arange(elems, dtype=jnp.int32)
    same_owner = targets[:, None] == targets[None, :]
    slot_rows = jnp.arange(rows, dtype=jnp.int32)[:, None]
    keys = targets * aggs + agg_local
    same_key = keys[:, None] == keys[None, :]
    firstidx = jnp.min(jnp.where(same_key, order[None, :], elems), 1)
    first = firstidx == order
    before = first[None, :] & same_owner & (order[None, :] < firstidx[:, None])
    position = targets * cap + jnp.sum(before.astype(jnp.int32), 1)
    placing = slot_rows == position[None, :]
    leading = (placing & first[None, :]).astype(jnp.int32)
    labels = jnp.sum(leading * (agg_local[None, :] + 1), 1) - 1
    weighted = jnp.einsum("eki,efkj->efij", p_blocks, applied, preferred_element_type=jnp.float32)
    mixing = (
        placing.astype(jnp.float32)[:, None, :, None]
        * jnp.transpose(slot_table(coarse_slot), (2, 0, 1))[None, :, :, :]
    )
    send_terms = jnp.einsum(
        "rsef,efij->rsij", mixing, weighted, precision=lax.Precision.HIGHEST
    ).astype(jnp.bfloat16)
    got_terms, got_labels = (
        lax.all_to_all(send_terms, "dev", split_axis=0, concat_axis=0, tiled=True),
        lax.all_to_all(labels, "dev", split_axis=0, concat_axis=0, tiled=True),
    )
    matching = (got_labels[:, None] == jnp.arange(aggs, dtype=jnp.int32)[None, :]).astype(
        jnp.bfloat16
    )
    coarse = jnp.einsum("ra,rsij->asij", matching, got_terms, preferred_element_type=jnp.float32)
    return coarse.astype(jnp.bfloat16)


def solution(mesh):
    placed = (
        P(("grp", "dev"), None, None, None),
        P(("grp", "dev"), None, None),
        P(("grp", "dev"), None),
        P(("grp", "dev"), None),
        P(("grp", "dev"), None),
        P(("grp", "dev")),
    )
    return jax.shard_map(
        on_device,
        mesh=mesh,
        in_specs=placed,
        out_specs=P(("grp", "dev"), None, None, None),
        check_vma=False,
    )
```

profile of v0, /device:TPU:22, one launch (start us, length us, event | category | flops | bytes accessed | tf_op | source)
XLA Modules:
  0.0 548.8 jit_solution(13377463529046650305)
XLA Ops:
  0.0 2.0 collective-permute-start.1
  2.1 2.4 collective-permute-start
  4.5 0.7 broadcast_add_fusion.1
  5.1 0.2 select_reduce_fusion.1
  5.3 9.3 %collective-permute-done.1 = bf16[1,1,32,128,128]{4,3,2,1,0:T(8,128)(2,1)S(1)} collective-permute-done((bf16[1,1,32,128,128]{4,3,2,1,0:T(8,128)(2,1)}, bf16[1,1,32,128,128]{4,3,2,1,0:T(8,128)(2,1)S(1)}, u32[]{:S(2)}, u32[]{:S(2)}) %collective-permute-start.1) | collective-permute-done | bytes 1048608 | tf_op jit(solution)/shard_map/ppermute | solution.py:17
  14.7 3.7 collective-permute-done
  18.4 1.0 copy-done.1
  19.4 3.2 pad_maximum_fusion
  22.6 2.7 collective-permute-start.3
  25.3 0.9 convert_reduce_fusion
  26.2 5.2 collective-permute-start.2
  31.5 0.7 multiply_add_fusion.1
  32.2 0.7 sub.7
  32.9 11.3 %all-to-all-start = ((s32[32,2,1]{1,2,0:T(1,128)}), s32[32,2,1]{1,2,0:T(1,128)S(1)}, u32[]{:S(2)}, u32[]{:S(2)}) async-start(s32[32,2,1]{1,2,0:T(1,128)} %bitcast.1), calls=%async_computation | async-start | bytes 32768 | tf_op jit(solution)/shard_map/all_to_all | solution.py:73
  44.2 2.3 copy.30
  46.5 0.7 gather_fusion.1
  47.3 0.7 copy.32
  48.0 1.7 gather_fusion
  49.6 1.6 copy.31
  51.4 1.2 fusion.30
  52.6 2.5 bitcast_dynamic-update-slice_fusion.6
  55.2 1.3 bitcast_dynamic-update-slice_fusion.5
  56.4 1.3 bitcast_dynamic-update-slice_fusion.4
  57.7 2.0 gather_fusion.5
  59.7 0.7 copy.36
  60.4 2.9 gather_fusion.4
  63.2 1.6 copy.35
  64.9 31.4 %collective-permute-done.3 = bf16[3,1,32,128,128]{4,3,2,1,0:T(8,128)(2,1)} collective-permute-done((bf16[3,1,32,128,128]{4,3,2,1,0:T(8,128)(2,1)}, bf16[3,1,32,128,128]{4,3,2,1,0:T(8,128)(2,1)}, u32[]{:S(2)}, u32[]{:S(2)}) %collective-permute-start.3) | collective-permute-done | bytes 3145760 | tf_op jit(solution)/shard_map/ppermute | solution.py:17
  96.3 2.3 slice_bitcast_fusion
  98.6 2.9 gather_fusion.3
  101.5 2.3 copy.34
  103.8 2.3 slice_bitcast_fusion.1
  106.1 2.9 gather_fusion.2
  109.0 2.3 copy.33
  111.2 2.5 bitcast_dynamic-update-slice_fusion.3
  113.7 2.5 bitcast_dynamic-update-slice_fusion.2
  116.2 1.3 bitcast_dynamic-update-slice_fusion.1
  117.5 1.3 bitcast_dynamic-update-slice_fusion
  118.8 13.4 %convolution_bitcast_fusion = f32[32,7,128,128]{2,3,1,0:T(8,128)} fusion(bf16[32,7,128,128]{2,3,1,0:T(8,128)(2,1)} %bitcast_dynamic-update-slice_fusion, bf16[32,7,128,128]{3,2,1,0:T(8,128)(2,1)} %param.8, bf16[32,128,128]{2,1,0:T(8,128)(2,1)S(1)} %copy-done), kind=kOutput, calls=%fused_computation.11 | convolution fusion | flops 1882718208 | bytes 30408704 | tf_op jit(solution)/shard_map/eki,efkj->efij/dot_general | solution.py:63
  132.2 16.5 %copy.37 = f32[32,7,128,128]{3,0,1,2:T(8,128)} copy(f32[32,7,128,128]{2,3,1,0:T(8,128)} %convolution_bitcast_fusion) | data formatting | bytes 29360128 | tf_op jit(solution)/shard_map/eki,efkj->efij/transpose | solution.py:63
  148.7 26.8 %bitcast_convert_fusion = bf16[64,7,128,128]{3,0,2,1:T(8,128)(2,1)S(1)} fusion(f32[32,7,128,128]{3,0,1,2:T(8,128)} %copy.37, f32[64,7,32,7,1]{0,2,3,4,1:T(8,128)S(1)} %copy-done.3), kind=kOutput, calls=%fused_computation.6 | convolution fusion | flops 19737346048 | bytes 29761536 | tf_op jit(solution)/shard_map/rsef,efij->rsij/dot_general | solution.py:68
  175.5 10.6 %copy.38 = bf16[64,7,128,128]{3,2,1,0:T(8,128)(2,1)} copy(bf16[64,7,128,128]{3,0,2,1:T(8,128)(2,1)S(1)} %bitcast_convert_fusion) | data formatting | bytes 29360128 | tf_op jit(solution)/shard_map/convert_element_type | solution.py:70
  186.1 11.4 %all-to-all-start.1 = ((bf16[64,7,128,128]{3,2,1,0:T(8,128)(2,1)}), bf16[64,7,128,128]{3,2,1,0:T(8,128)(2,1)}, u32[]{:S(2)}, u32[]{:S(2)}) async-start(bf16[64,7,128,128]{3,2,1,0:T(8,128)(2,1)} %copy.38), calls=%async_computation.1 | async-start | bytes 29360128 | tf_op jit(solution)/shard_map/all_to_all | solution.py:72
  197.5 0.5 broadcast.77
  198.0 0.7 reduce.3
  198.8 335.3 %all-to-all-done.1 = bf16[64,7,128,128]{3,2,1,0:T(8,128)(2,1)} async-done(((bf16[64,7,128,128]{3,2,1,0:T(8,128)(2,1)}), bf16[64,7,128,128]{3,2,1,0:T(8,128)(2,1)}, u32[]{:S(2)}, u32[]{:S(2)}) %all-to-all-start.1) | async-done | bytes 14680096 | tf_op jit(solution)/shard_map/all_to_all | solution.py:72
  534.1 13.0 %fusion.10 = bf16[8,7,128,128]{3,0,2,1:T(8,128)(2,1)S(1)} fusion(bf16[64,7,128,128]{3,2,1,0:T(8,128)(2,1)} %all-to-all-done.1, s32[64]{0:T(128)S(1)} %eq.93), kind=kOutput, calls=%fused_computation.16 | convolution fusion | flops 118358528 | bytes 16515328 | tf_op jit(solution)/shard_map/ra,rsij->asij/dot_general | solution.py:78
  547.1 1.7 copy.40
  (25 shorter events, 0.4 us)
Async XLA Ops:
  0.0 46.5 %copy-start = (bf16[32,128,128]{2,1,0:T(8,128)(2,1)S(1)}, bf16[32,128,128]{2,1,0:T(8,128)(2,1)}, u32[]{:S(2)}) copy-start(bf16[32,128,128]{2,1,0:T(8,128)(2,1)} %param.9) | copy-start | bytes 3145732
  0.0 46.5 %copy-start.5 = (s32[32,6]{0,1:T(8,128)S(1)}, s32[32,6]{0,1:T(8,128)}, u32[]{:S(2)}) copy-start(s32[32,6]{0,1:T(8,128)} %param.10) | copy-start | bytes 2308
  0.0 14.7 %collective-permute-start.1 = (bf16[1,1,32,128,128]{4,3,2,1,0:T(8,128)(2,1)}, bf16[1,1,32,128,128]{4,3,2,1,0:T(8,128)(2,1)S(1)}, u32[]{:S(2)}, u32[]{:S(2)}) collective-permute-start(bf16[1,1,32,128,128]{4,3,2,1,0:T(8,128)(2,1)} %bitcast.80), channel_id=1, source_target_pairs={{32,0},{64,32},{96,64},{128,96},{160,128},{192,160},{224,192},{33,... | collective-permute-start | bytes 3145736 | tf_op jit(solution)/shard_map/ppermute | solution.py:17
  2.1 16.3 %collective-permute-start = (bf16[1,1,32,128,128]{4,3,2,1,0:T(8,128)(2,1)}, bf16[1,1,32,128,128]{4,3,2,1,0:T(8,128)(2,1)S(1)}, u32[]{:S(2)}, u32[]{:S(2)}) collective-permute-start(bf16[1,1,32,128,128]{4,3,2,1,0:T(8,128)(2,1)} %bitcast.81), channel_id=1, source_target_pairs={{0,32},{32,64},{64,96},{96,128},{128,160},{160,192},{192,224},{1,3... | collective-permute-start | bytes 3145736 | tf_op jit(solution)/shard_map/ppermute | solution.py:14
  5.3 46.1 %copy-start.4 = (s32[32,7]{0,1:T(8,128)S(1)}, s32[32,7]{0,1:T(8,128)}, u32[]{:S(2)}) copy-start(s32[32,7]{0,1:T(8,128)} %param.11) | copy-start | bytes 2692
  14.7 7.9 %copy-start.2 = (bf16[1,1,32,128,128]{4,3,2,1,0:T(8,128)(2,1)}, bf16[1,1,32,128,128]{4,3,2,1,0:T(8,128)(2,1)S(1)}, u32[]{:S(2)}) copy-start(bf16[1,1,32,128,128]{4,3,2,1,0:T(8,128)(2,1)S(1)} %collective-permute-done.1) | copy-start | bytes 3145732
  18.4 1.0 copy-start.1
  22.6 73.7 %collective-permute-start.3 = (bf16[3,1,32,128,128]{4,3,2,1,0:T(8,128)(2,1)}, bf16[3,1,32,128,128]{4,3,2,1,0:T(8,128)(2,1)}, u32[]{:S(2)}, u32[]{:S(2)}) collective-permute-start(bf16[3,1,32,128,128]{4,3,2,1,0:T(8,128)(2,1)} %pad_maximum_fusion), channel_id=1, source_target_pairs={{1,0},{2,1},{3,2},{4,3},{5,4},{6,5},{7,6},{8,7},{9,8},{10,9},{11,1... | collective-permute-start | bytes 9437192 | tf_op jit(solution)/shard_map/ppermute | solution.py:17
  26.2 77.6 %collective-permute-start.2 = (bf16[3,1,32,128,128]{4,3,2,1,0:T(8,128)(2,1)}, bf16[3,1,32,128,128]{4,3,2,1,0:T(8,128)(2,1)}, u32[]{:S(2)}, u32[]{:S(2)}) collective-permute-start(bf16[3,1,32,128,128]{4,3,2,1,0:T(8,128)(2,1)} %pad_maximum_fusion), channel_id=1, source_target_pairs={{0,1},{1,2},{2,3},{3,4},{4,5},{5,6},{6,7},{7,8},{8,9},{9,10},{10,1... | collective-permute-start | bytes 9437192 | tf_op jit(solution)/shard_map/ppermute | solution.py:14
  32.9 153.2 %all-to-all-start = ((s32[32,2,1]{1,2,0:T(1,128)}), s32[32,2,1]{1,2,0:T(1,128)S(1)}, u32[]{:S(2)}, u32[]{:S(2)}) async-start(s32[32,2,1]{1,2,0:T(1,128)} %bitcast.1), calls=%async_computation | async-start | bytes 32768 | tf_op jit(solution)/shard_map/all_to_all | solution.py:73
  132.2 16.5 %copy-start.3 = (f32[64,7,32,7,1]{0,2,3,4,1:T(8,128)S(1)}, f32[64,7,32,7,1]{0,2,3,4,1:T(8,128)}, u32[]{:S(2)}) copy-start(f32[64,7,32,7,1]{0,2,3,4,1:T(8,128)} %fusion.30) | copy-start | bytes 1204228
  186.1 348.0 %all-to-all-start.1 = ((bf16[64,7,128,128]{3,2,1,0:T(8,128)(2,1)}), bf16[64,7,128,128]{3,2,1,0:T(8,128)(2,1)}, u32[]{:S(2)}, u32[]{:S(2)}) async-start(bf16[64,7,128,128]{3,2,1,0:T(8,128)(2,1)} %copy.38), calls=%async_computation.1 | async-start | bytes 29360128 | tf_op jit(solution)/shard_map/all_to_all | solution.py:72
where the time goes:
time: 553 us; the launch traced here: 549 us
  waiting for transfers between devices  380 us (69%)
  local copies, waits for them, and re-layouts  62.6 us (11%)
  matrix products  53.3 us (10%)
  starting transfers between devices  35.1 us (6%)
  other arithmetic  17.9 us (3%)
    all_to_all x1, waiting for transfers between devices, on_device(): lax.all_to_all(send_terms, 'dev', split_axis=0, concat_axis=0, tiled=True)  335 us
    ppermute x2, waiting for transfers between devices, with_halo(): lax.ppermute(lax.slice_in_dim(block, 0, width, axis=dim), axis, backward)  40.8 us
    dot_general x1, matrix products, on_device(): jnp.einsum('rsef,efij->rsij', mixing, weighted, precision=lax.Precision.H...  26.8 us
    gather x12, local copies, waits for them, and re-layouts, on_device(): jnp.take(sources[face], neighbours[:, face], axis=0)  22.1 us
    transpose x1, local copies, waits for them, and re-layouts, on_device(): jnp.einsum('eki,efkj->efij', p_blocks, applied, preferred_element_type=jn...  16.5 us
    dot_general x1, matrix products, on_device(): jnp.einsum('eki,efkj->efij', p_blocks, applied, preferred_element_type=jn...  13.4 us
    dot_general x1, matrix products, on_device(): jnp.einsum('ra,rsij->asij', matching, got_terms, preferred_element_type=j...  13 us
    all_to_all x1, starting transfers between devices, on_device(): lax.all_to_all(send_terms, 'dev', split_axis=0, concat_axis=0, tiled=True)  11.4 us
  transfers between devices with their start and end apart: 6, of which 4 were waited for; matrix products, arithmetic and copies ran while one was open for 21% of the time, Pallas kernels for 0%

commit v1 on v0

v1 whole, which is shorter than its diff:
```python
import jax
import jax.numpy as jnp
from jax import lax
from jax.experimental import pallas as pl
from jax.experimental.pallas import tpu as pltpu
from jax.sharding import PartitionSpec as P

KC = 7
NX = 4
NZ = 8
AGG = 8
EB = 4
PIECES = 2
MESH = pl.DeviceIdType.MESH
BF = jnp.bfloat16
F32 = jnp.float32

RELS = (4, 3, 5, 2, 6, 1, 7, 0)
ORDER = tuple(
    (t, p)
    for group in ((0,), (1, 2), (3, 4), (5, 6), (7,))
    for p in range(PIECES)
    for t in group
)
ZOFF = {4: 0, 3: 4, 2: 12, 1: 20}
ZROWS = 28


def halo(p_blocks, axis, up):
    count = lax.axis_size(axis)
    perm = [(i, i + 1) if up else (i + 1, i) for i in range(count - 1)]
    return lax.ppermute(p_blocks, axis, perm)


def rows_kernel(near, slot, pos, a_ref, p_ref, dl_ref, dh_ref, gl_ref, gh_ref, s_hbm, rows, sems):
    step = pl.program_id(0)
    sources = (p_ref, p_ref, dl_ref, dh_ref, gl_ref, gh_ref)
    for j in range(EB):
        e = step * EB + j
        own = p_ref[e]
        faces = [own] + [sources[f][near[e * 6 + f]] for f in range(6)]
        applied = [
            jnp.dot(a_ref[j, f], faces[f], preferred_element_type=F32).astype(BF)
            for f in range(KC)
        ]
        weighted = [
            lax.dot_general(own, w, (((0,), (0,)), ((), ())), preferred_element_type=F32)
            for w in applied
        ]
        for s in range(KC):
            total = None
            for f in range(KC):
                term = jnp.where(slot[e * KC + f] == s, weighted[f], 0.0)
                total = term if total is None else total + term
            rows[e, s] = total.astype(BF)
        pltpu.make_async_copy(rows.at[e], s_hbm.at[pos[e]], sems.at[e]).start()

    @pl.when(step == pl.num_programs(0) - 1)
    def _():
        def finish(e, carry):
            pltpu.make_async_copy(rows.at[e], s_hbm.at[pos[e]], sems.at[e]).wait()
            return carry

        lax.fori_loop(0, rows.shape[0], finish, 0)


def make_rows(a_blocks, p_blocks, low_d, high_d, low_g, high_g, near, slot, pos):
    elems, _, blk, _ = a_blocks.shape
    full = pl.BlockSpec((elems, blk, blk), lambda i, *_: (0, 0, 0), pipeline_mode=pl.Buffered(1))
    return pl.pallas_call(
        rows_kernel,
        grid_spec=pltpu.PrefetchScalarGridSpec(
            num_scalar_prefetch=3,
            grid=(elems // EB,),
            in_specs=[pl.BlockSpec((EB, KC, blk, blk), lambda i, *_: (i, 0, 0, 0))] + [full] * 5,
            out_specs=pl.BlockSpec(memory_space=pl.ANY),
            scratch_shapes=[
                pltpu.VMEM((elems, KC, blk, blk), BF),
                pltpu.SemaphoreType.DMA((elems,)),
            ],
        ),
        out_shape=jax.ShapeDtypeStruct((2 * NX * NZ, KC, blk, blk), BF),
        compiler_params=pltpu.CompilerParams(vmem_limit_bytes=40 << 20),
        name="rows",
    )(near, slot, pos, a_blocks, p_blocks, low_d, high_d, low_g, high_g)


def exchange_kernel(
    labels, s_hbm, out, own, left, right, opp, relay, zs, zr,
    own_sem, x_send, x_recv, z_send, z_recv,
):
    blk = out.shape[2]
    part = blk // PIECES
    g = lax.axis_index("grp")
    d = lax.axis_index("dev")
    z = d // NX
    x = d % NX
    xr = (g, z * NX + (x + 1) % NX)
    xl = (g, z * NX + (x + NX - 1) % NX)
    zu = (g, ((z + 1) % NZ) * NX + x)
    zd = (g, ((z + NZ - 1) % NZ) * NX + x)

    barrier = pltpu.get_barrier_semaphore()
    for peer in (xr, xl, zu, zd):
        pl.semaphore_signal(barrier, inc=1, device_id=peer, device_id_type=MESH)
    pl.semaphore_wait(barrier, 4)

    def base(t, dx):
        return 2 * (((z + RELS[t]) % NZ) * NX + (x + dx) % NX)

    def rows_of(p):
        return pl.ds(p * part, part)

    def remote(kind, t, p, src, dst, peer):
        n = t * PIECES + p
        return pltpu.make_async_remote_copy(
            src_ref=src,
            dst_ref=dst,
            send_sem=x_send.at[kind, n],
            recv_sem=x_recv.at[kind, n],
            device_id=peer,
            device_id_type=MESH,
        )

    def first_hop(t, p):
        r = rows_of(p)
        two = pl.ds(2 * t, 2)
        return (
            remote(0, t, p, s_hbm.at[base(t, 2), :, r], relay.at[2 * t, :, r], xr),
            remote(1, t, p, s_hbm.at[base(t, 2) + 1, :, r], relay.at[2 * t + 1, :, r], xl),
            remote(2, t, p, s_hbm.at[pl.ds(base(t, 1), 2), :, r], left.at[two, :, r], xr),
            remote(3, t, p, s_hbm.at[pl.ds(base(t, 3), 2), :, r], right.at[two, :, r], xl),
        )

    def second_hop(t, p):
        r = rows_of(p)
        return (
            remote(4, t, p, relay.at[2 * t, :, r], opp.at[2 * t, :, r], xr),
            remote(5, t, p, relay.at[2 * t + 1, :, r], opp.at[2 * t + 1, :, r], xl),
        )

    def own_copy(t):
        return pltpu.make_async_copy(
            s_hbm.at[pl.ds(base(t, 0), 2)], own.at[pl.ds(2 * t, 2)], own_sem.at[t]
        )

    def z_copy(way, k, p):
        n = (way * 4 + k - 1) * PIECES + p
        rows = pl.ds(ZOFF[k], 4 if k == 4 else AGG)
        return pltpu.make_async_remote_copy(
            src_ref=zs.at[way, rows, :, rows_of(p)],
            dst_ref=zr.at[way, rows, :, rows_of(p)],
            send_sem=z_send.at[n],
            recv_sem=z_recv.at[n],
            device_id=zu if way == 0 else zd,
            device_id_type=MESH,
        )

    def combine(t, p, first, count, arrived, put):
        r = rows_of(p)
        names = [
            labels[src * 2 * NX * NZ + base(t, 0) + k] for src in range(4) for k in range(2)
        ]

        def one(i, carry):
            a = first + i
            picks = [name == a for name in names]

            def slot(s, inner):
                total = None
                for ref in arrived:
                    term = ref(i, s).astype(F32)
                    total = term if total is None else total + term
                n = 0
                for ref in (own, left, right, opp):
                    for k in range(2):
                        term = jnp.where(picks[n], ref[2 * t + k, s, r].astype(F32), 0.0)
                        total = term if total is None else total + term
                        n += 1
                put(i, s, total.astype(BF))
                return inner

            return lax.fori_loop(0, KC, slot, carry)

        lax.fori_loop(0, count, one, 0)

    def from_z(way, row, p):
        return lambda i, s: zr[way, row + i, s, rows_of(p)]

    def to_z(way, row, p):
        def put(i, s, value):
            zs[way, row + i, s, rows_of(p)] = value

        return put

    def step(t, p):
        rel = RELS[t]
        if rel == 4:
            combine(t, p, 0, 4, (), to_z(0, 0, p))
            z_copy(0, 4, p).start()
            combine(t, p, 4, 4, (), to_z(1, 0, p))
            z_copy(1, 4, p).start()
        elif rel == 0:
            for way in range(2):
                z_copy(way, 1, p).wait_recv()

            def put(i, s, value):
                out[i, s, rows_of(p)] = value

            combine(t, p, 0, AGG, (from_z(0, ZOFF[1], p), from_z(1, ZOFF[1], p)), put)
        else:
            way, k = (0, rel) if rel < 4 else (1, NZ - rel)
            z_copy(way, k + 1, p).wait_recv()
            if k == 3:
                lower = (from_z(0, 0, p),) if way == 0 else ()
                upper = (from_z(1, 0, p),) if way == 1 else ()
                combine(t, p, 0, 4, lower, to_z(way, ZOFF[3], p))
                combine(t, p, 4, 4, upper, to_z(way, ZOFF[3] + 4, p))
            else:
                combine(t, p, 0, AGG, (from_z(way, ZOFF[k + 1], p),), to_z(way, ZOFF[k], p))
            z_copy(way, k, p).start()

    for copy in first_hop(*ORDER[0]):
        copy.start()
    for t in range(NZ):
        own_copy(t).start()
    for n, (t, p) in enumerate(ORDER):
        hop = first_hop(t, p)
        again = second_hop(t, p)
        for way in range(2):
            hop[way].wait_recv()
            again[way].start()
        if n + 1 < len(ORDER):
            for copy in first_hop(*ORDER[n + 1]):
                copy.start()
        if p == 0:
            own_copy(t).wait()
        hop[2].wait_recv()
        hop[3].wait_recv()
        again[0].wait_recv()
        again[1].wait_recv()
        step(t, p)
    for t, p in ORDER:
        for copy in first_hop(t, p) + second_hop(t, p):
            copy.wait_send()
    for way in range(2):
        for k in range(1, 5):
            for p in range(PIECES):
                z_copy(way, k, p).wait_send()


def exchange(labels, rows):
    _, _, blk, _ = rows.shape
    block = (KC, blk, blk)
    n = NZ * PIECES
    return pl.pallas_call(
        exchange_kernel,
        in_specs=[
            pl.BlockSpec(memory_space=pltpu.SMEM),
            pl.BlockSpec(memory_space=pl.ANY),
        ],
        out_specs=pl.BlockSpec(memory_space=pltpu.VMEM),
        out_shape=jax.ShapeDtypeStruct((AGG,) + block, BF),
        scratch_shapes=[
            pltpu.VMEM((2 * NZ,) + block, BF),
            pltpu.VMEM((2 * NZ,) + block, BF),
            pltpu.VMEM((2 * NZ,) + block, BF),
            pltpu.VMEM((2 * NZ,) + block, BF),
            pltpu.VMEM((2 * NZ,) + block, BF),
            pltpu.VMEM((2, ZROWS) + block, BF),
            pltpu.VMEM((2, ZROWS) + block, BF),
            pltpu.SemaphoreType.DMA((NZ,)),
            pltpu.SemaphoreType.DMA((6, n)),
            pltpu.SemaphoreType.DMA((6, n)),
            pltpu.SemaphoreType.DMA((n,)),
            pltpu.SemaphoreType.DMA((n,)),
        ],
        compiler_params=pltpu.CompilerParams(
            collective_id=0, has_side_effects=True, vmem_limit_bytes=58 << 20
        ),
        name="exchange",
    )(labels, rows)


def on_device(a_blocks, p_blocks, neighbours, coarse_slot, owner, agg_local):
    elems = p_blocks.shape[0]
    low_d, high_d = halo(p_blocks, "dev", True), halo(p_blocks, "dev", False)
    low_g, high_g = halo(p_blocks, "grp", True), halo(p_blocks, "grp", False)
    targets = owner[:, 0]
    order = jnp.arange(elems, dtype=jnp.int32)
    earlier = (targets[:, None] == targets[None, :]) & (order[None, :] < order[:, None])
    pos = 2 * targets + jnp.sum(earlier.astype(jnp.int32), 1)
    holds = jnp.arange(2 * NX * NZ, dtype=jnp.int32)[:, None] == pos[None, :]
    labels = jnp.sum(jnp.where(holds, agg_local[None, :] + 1, 0), 1) - 1

    def from_x(step):
        perm = [
            (z * NX + x, z * NX + (x + step) % NX) for z in range(NZ) for x in range(NX)
        ]
        return lax.ppermute(labels, "dev", perm)

    all_labels = jnp.concatenate([labels, from_x(1), from_x(NX - 1), from_x(2)])
    rows = make_rows(
        a_blocks, p_blocks, low_d, high_d, low_g, high_g,
        neighbours.reshape(-1), coarse_slot.reshape(-1), pos,
    )
    return exchange(all_labels, rows)


def solution(mesh):
    placed = (
        P(("grp", "dev"), None, None, None),
        P(("grp", "dev"), None, None),
        P(("grp", "dev"), None),
        P(("grp", "dev"), None),
        P(("grp", "dev"), None),
        P(("grp", "dev")),
    )
    return jax.shard_map(
        on_device,
        mesh=mesh,
        in_specs=placed,
        out_specs=P(("grp", "dev"), None, None, None),
        check_vma=False,
    )
```

time: 553 us -> 237 us (0.43)
  waiting for transfers between devices: 380 us -> 17.9 us
  Pallas kernels: 0 us -> 187 us
  local copies, waits for them, and re-layouts: 62.6 us -> 9.01 us
  matrix products: 53.3 us -> 0 us
  starting transfers between devices: 35.1 us -> 18.7 us
  other arithmetic: 17.9 us -> 2.97 us
    all_to_all x2 -> x0, waiting for transfers between devices: 335 us -> none  [the longest x1 335 us: on_device(): lax.all_to_all(send_terms, 'dev', split_axis=0, concat_axis=0, tiled=True)]
    pallas_call x0 -> x2, Pallas kernels: none -> 187 us  [the longest x1 171 us: exchange(): pl.pallas_call(exchange_kernel, in_specs=[pl.BlockSpec(memory_space=pltpu...]
    dot_general x3 -> x0, matrix products: 53.3 us -> none  [the longest x1 26.8 us: on_device(): jnp.einsum('rsef,efij->rsij', mixing, weighted, precision=lax.Precision.H...]
    ppermute x4 -> x7, waiting for transfers between devices: 44.5 us -> 17.9 us  [the longest x3 17.9 us: from_x(): return lax.ppermute(labels, 'dev', perm)]
    all_to_all x2 -> x0, starting transfers between devices: 22.7 us -> none  [the longest x1 11.4 us: on_device(): lax.all_to_all(send_terms, 'dev', split_axis=0, concat_axis=0, tiled=True)]
    gather x12 -> x0, local copies, waits for them, and re-layouts: 22.1 us -> none  [on_device(): jnp.take(sources[face], neighbours[:, face], axis=0)]
    transpose x1 -> x0, local copies, waits for them, and re-layouts: 16.5 us -> none  [on_device(): jnp.einsum('eki,efkj->efij', p_blocks, applied, preferred_element_type=jn...]
    convert_element_type x2 -> x0, local copies, waits for them, and re-layouts: 12.3 us -> none  [the longest x1 10.6 us: on_device(): send_terms = jnp.einsum('rsef,efij->rsij', mixing, weighted, precision=la...]
  transfers between devices with their start and end apart: 6 -> 7, of which waited for: 4 -> 2; matrix products, arithmetic and copies ran while one was open for 21% -> 2% of each run, Pallas kernels for 0% -> 0%
where the time goes in v1:
time: 237 us; the launch traced here: 236 us
  Pallas kernels  187 us (79%)
  starting transfers between devices  18.7 us (8%)
  waiting for transfers between devices  17.9 us (8%)
  local copies, waits for them, and re-layouts  9.01 us (4%)
  other arithmetic  2.97 us (1%)
    pallas_call x1, Pallas kernels, exchange(): pl.pallas_call(exchange_kernel, in_specs=[pl.BlockSpec(memory_space=pltpu...  171 us
    ppermute x3, waiting for transfers between devices, from_x(): return lax.ppermute(labels, 'dev', perm)  17.9 us
    pallas_call x1, Pallas kernels, make_rows(): pl.pallas_call(rows_kernel, grid_spec=pltpu.PrefetchScalarGridSpec(num_sc...  15.9 us
    ppermute x4, starting transfers between devices, halo(): return lax.ppermute(p_blocks, axis, perm)  13 us
    unnamed x7, local copies, waits for them, and re-layouts  8.81 us
    ppermute x3, starting transfers between devices, from_x(): return lax.ppermute(labels, 'dev', perm)  5.73 us
  transfers between devices with their start and end apart: 7, of which 2 were waited for; matrix products, arithmetic and copies ran while one was open for 2% of the time, Pallas kernels for 0%

profile of v1, /device:TPU:22, one launch (start us, length us, event | category | flops | bytes accessed | tf_op | source)
XLA Modules:
  0.0 236.0 jit_solution(4317741249808862042)
XLA Ops:
  0.0 1.9 collective-permute-start.5
  1.9 2.7 %collective-permute-start.4 = (bf16[32,128,128]{2,1,0:T(8,128)(2,1)}, bf16[32,128,128]{2,1,0:T(8,128)(2,1)S(1)}, u32[]{:S(2)}, u32[]{:S(2)}) collective-permute-start(bf16[32,128,128]{2,1,0:T(8,128)(2,1)} %p_ref.1), channel_id=1, source_target_pairs={{1,0},{2,1},{3,2},{4,3},{5,4},{6,5},{7,6},{8,7},{9,8},{10,9},{11,1... | collective-permute-start | bytes 3145736 | tf_op jit(solution)/shard_map/ppermute | solution.py:32
  4.7 5.2 %collective-permute-start.3 = (bf16[32,128,128]{2,1,0:T(8,128)(2,1)}, bf16[32,128,128]{2,1,0:T(8,128)(2,1)S(1)}, u32[]{:S(2)}, u32[]{:S(2)}) collective-permute-start(bf16[32,128,128]{2,1,0:T(8,128)(2,1)} %p_ref.1), channel_id=1, source_target_pairs={{0,1},{1,2},{2,3},{3,4},{4,5},{5,6},{6,7},{7,8},{8,9},{9,10},{10,1... | collective-permute-start | bytes 3145736 | tf_op jit(solution)/shard_map/ppermute | solution.py:32
  9.9 3.1 %collective-permute-start.6 = (bf16[32,128,128]{2,1,0:T(8,128)(2,1)}, bf16[32,128,128]{2,1,0:T(8,128)(2,1)}, u32[]{:S(2)}, u32[]{:S(2)}) collective-permute-start(bf16[32,128,128]{2,1,0:T(8,128)(2,1)} %p_ref.1), channel_id=1, source_target_pairs={{32,0},{64,32},{96,64},{128,96},{160,128},{192,160},{224,192},{33,... | collective-permute-start | bytes 3145736 | tf_op jit(solution)/shard_map/ppermute | solution.py:32
  13.0 0.9 convert_reduce_fusion
  13.9 0.7 broadcast_add_fusion.1
  14.6 0.7 multiply_add_fusion.pos
  15.2 0.1 select_reduce_fusion
  15.3 0.1 collective-permute-start.2
  15.4 14.2 %collective-permute-done.2 = s32[64]{0:T(128)S(1)} collective-permute-done((s32[64]{0:T(128)S(1)}, s32[64]{0:T(128)S(1)}, u32[]{:S(2)}, u32[]{:S(2)}) %collective-permute-start.2) | collective-permute-done | bytes 288 | tf_op jit(solution)/shard_map/ppermute | solution.py:300
  29.6 3.6 %collective-permute-start.1 = (s32[64]{0:T(128)S(1)}, s32[64]{0:T(128)S(1)}, u32[]{:S(2)}, u32[]{:S(2)}) collective-permute-start(s32[64]{0:T(128)S(1)} %broadcast_add_fusion), channel_id=1, source_target_pairs={{0,3},{1,0},{2,1},{3,2},{4,7},{5,4},{6,5},{7,6},{8,11},{9,8},{10,9... | collective-permute-start | bytes 776 | tf_op jit(solution)/shard_map/ppermute | solution.py:300
  33.2 3.7 %collective-permute-done.1 = s32[64]{0:T(128)S(1)} collective-permute-done((s32[64]{0:T(128)S(1)}, s32[64]{0:T(128)S(1)}, u32[]{:S(2)}, u32[]{:S(2)}) %collective-permute-start.1) | collective-permute-done | bytes 288 | tf_op jit(solution)/shard_map/ppermute | solution.py:300
  36.9 2.0 collective-permute-start
  38.9 0.8 copy.9
  39.7 0.1 reshape.17.near
  39.8 0.8 copy.10
  40.6 0.1 reshape.18.slot
  40.7 0.0 collective-permute-done
  40.7 0.6 pad_add_fusion.labels
  41.3 0.0 collective-permute-done.5.gl_ref
  41.3 0.0 collective-permute-done.4.dh_ref
  41.3 0.0 collective-permute-done.3.dl_ref
  41.3 0.0 collective-permute-done.6.gh_ref
  41.3 0.0 copy-start
  41.4 3.1 %copy-done = bf16[32,7,128,128]{3,2,1,0:T(8,128)(2,1)S(1)} copy-done((bf16[32,7,128,128]{3,2,1,0:T(8,128)(2,1)S(1)}, bf16[32,7,128,128]{3,2,1,0:T(8,128)(2,1)}, u32[]{:S(2)}) %copy-start) | copy-done | bytes 7340056
  44.5 0.0 copy-start.1
  44.5 1.2 copy-done.1
  45.7 15.9 %rows.1.s_hbm = bf16[64,7,128,128]{3,2,1,0:T(8,128)(2,1)} custom-call(s32[192]{0:T(256)S(1)} %reshape.17.near, s32[224]{0:T(256)S(1)} %reshape.18.slot, s32[32]{0:T(128)S(1)} %multiply_add_fusion.pos, bf16[32,7,128,128]{3,2,1,0:T(8,128)(2,1)S(1)} %copy-done, bf16[32,128,128]{2,1,0:T(8,128)(2,1)S(1)} %copy-done.1, ...), custom_call_target="tpu_custom_call" | custom-call | tf_op jit(solution)/shard_map/rows/pallas_call | solution.py:70
  61.6 171.5 %exchange.1 = bf16[8,7,128,128]{3,2,1,0:T(8,128)(2,1)} custom-call(s32[256]{0:T(256)} %pad_add_fusion.labels, bf16[64,7,128,128]{3,2,1,0:T(8,128)(2,1)} %rows.1.s_hbm), custom_call_target="tpu_custom_call" | custom-call | tf_op jit(solution)/shard_map/exchange/pallas_call | solution.py:256
  233.1 2.9 %copy.12 = bf16[8,7,128,128]{3,2,1,0:T(8,128)(2,1)} copy(bf16[8,7,128,128]{3,2,1,0:T(8,128)(2,1)} %exchange.1) | data formatting | bytes 3670016
  (1 shorter events, 0.0 us)
Async XLA Ops:
  0.0 41.3 %collective-permute-start.5 = (bf16[32,128,128]{2,1,0:T(8,128)(2,1)}, bf16[32,128,128]{2,1,0:T(8,128)(2,1)S(1)}, u32[]{:S(2)}, u32[]{:S(2)}) collective-permute-start(bf16[32,128,128]{2,1,0:T(8,128)(2,1)} %p_ref.1), channel_id=1, source_target_pairs={{0,32},{32,64},{64,96},{96,128},{128,160},{160,192},{192,224},{1,3... | collective-permute-start | bytes 3145736 | tf_op jit(solution)/shard_map/ppermute | solution.py:32
  1.9 39.4 %collective-permute-start.4 = (bf16[32,128,128]{2,1,0:T(8,128)(2,1)}, bf16[32,128,128]{2,1,0:T(8,128)(2,1)S(1)}, u32[]{:S(2)}, u32[]{:S(2)}) collective-permute-start(bf16[32,128,128]{2,1,0:T(8,128)(2,1)} %p_ref.1), channel_id=1, source_target_pairs={{1,0},{2,1},{3,2},{4,3},{5,4},{6,5},{7,6},{8,7},{9,8},{10,9},{11,1... | collective-permute-start | bytes 3145736 | tf_op jit(solution)/shard_map/ppermute | solution.py:32
  4.7 36.7 %collective-permute-start.3 = (bf16[32,128,128]{2,1,0:T(8,128)(2,1)}, bf16[32,128,128]{2,1,0:T(8,128)(2,1)S(1)}, u32[]{:S(2)}, u32[]{:S(2)}) collective-permute-start(bf16[32,128,128]{2,1,0:T(8,128)(2,1)} %p_ref.1), channel_id=1, source_target_pairs={{0,1},{1,2},{2,3},{3,4},{4,5},{5,6},{6,7},{7,8},{8,9},{9,10},{10,1... | collective-permute-start | bytes 3145736 | tf_op jit(solution)/shard_map/ppermute | solution.py:32
  9.9 31.4 %collective-permute-start.6 = (bf16[32,128,128]{2,1,0:T(8,128)(2,1)}, bf16[32,128,128]{2,1,0:T(8,128)(2,1)}, u32[]{:S(2)}, u32[]{:S(2)}) collective-permute-start(bf16[32,128,128]{2,1,0:T(8,128)(2,1)} %p_ref.1), channel_id=1, source_target_pairs={{32,0},{64,32},{96,64},{128,96},{160,128},{192,160},{224,192},{33,... | collective-permute-start | bytes 3145736 | tf_op jit(solution)/shard_map/ppermute | solution.py:32
  15.3 14.2 %collective-permute-start.2 = (s32[64]{0:T(128)S(1)}, s32[64]{0:T(128)S(1)}, u32[]{:S(2)}, u32[]{:S(2)}) collective-permute-start(s32[64]{0:T(128)S(1)} %broadcast_add_fusion), channel_id=1, source_target_pairs={{0,2},{1,3},{2,0},{3,1},{4,6},{5,7},{6,4},{7,5},{8,10},{9,11},{10,... | collective-permute-start | bytes 776 | tf_op jit(solution)/shard_map/ppermute | solution.py:300
  29.6 7.3 %collective-permute-start.1 = (s32[64]{0:T(128)S(1)}, s32[64]{0:T(128)S(1)}, u32[]{:S(2)}, u32[]{:S(2)}) collective-permute-start(s32[64]{0:T(128)S(1)} %broadcast_add_fusion), channel_id=1, source_target_pairs={{0,3},{1,0},{2,1},{3,2},{4,7},{5,4},{6,5},{7,6},{8,11},{9,8},{10,9... | collective-permute-start | bytes 776 | tf_op jit(solution)/shard_map/ppermute | solution.py:300
  36.9 3.8 %collective-permute-start = (s32[64]{0:T(128)S(1)}, s32[64]{0:T(128)S(1)}, u32[]{:S(2)}, u32[]{:S(2)}) collective-permute-start(s32[64]{0:T(128)S(1)} %broadcast_add_fusion), channel_id=1, source_target_pairs={{0,1},{1,2},{2,3},{3,0},{4,5},{5,6},{6,7},{7,4},{8,9},{9,10},{10,1... | collective-permute-start | bytes 776 | tf_op jit(solution)/shard_map/ppermute | solution.py:300
  41.3 3.1 %copy-start = (bf16[32,7,128,128]{3,2,1,0:T(8,128)(2,1)S(1)}, bf16[32,7,128,128]{3,2,1,0:T(8,128)(2,1)}, u32[]{:S(2)}) copy-start(bf16[32,7,128,128]{3,2,1,0:T(8,128)(2,1)} %a_ref.1) | copy-start | bytes 22020100
  44.5 1.2 copy-start.1

commit v2 on v1

v2 whole, which is shorter than its diff:
```python
import jax
import jax.numpy as jnp
from jax import lax
from jax.experimental import pallas as pl
from jax.experimental.pallas import tpu as pltpu
from jax.sharding import PartitionSpec as P

KC = 7
NX = 4
NZ = 8
AGG = 8
SLOTS = 2 * NX * NZ
PIECES = 2
RING = 4
MESH = pl.DeviceIdType.MESH
BF = jnp.bfloat16
F32 = jnp.float32
I32 = jnp.int32

RELS = (4, 3, 5, 2, 6, 1, 7, 0)
ORDER = tuple(
    (t, p)
    for group in ((0,), (1, 2), (3, 4), (5, 6), (7,))
    for p in range(PIECES)
    for t in group
)
ZIN = {4: 0, 3: 4, 2: 12, 1: 20}
ZIN_ROWS = 28
ZOUT = {4: 0, 3: 4, 2: 12, 1: 4}
ZOUT_ROWS = 20
SOURCE = (0, 0, 0, 1, 2, 3, 4)


def tables_kernel(owner, agg_local, elem, label, used):
    def clear(i, carry):
        elem[i] = 0
        label[0, i] = -1
        return carry

    def clear_used(i, carry):
        used[i] = 0
        return carry

    def place(e, carry):
        o = owner[0, e]
        r = 2 * o + used[o]
        used[o] = used[o] + 1
        elem[r] = e
        label[0, r] = agg_local[0, e]
        return carry

    lax.fori_loop(0, SLOTS, clear, 0)
    lax.fori_loop(0, SLOTS // 2, clear_used, 0)
    lax.fori_loop(0, owner.shape[1], place, 0)


def make_tables(owner, agg_local):
    smem = pl.BlockSpec(memory_space=pltpu.SMEM)
    return pl.pallas_call(
        tables_kernel,
        in_specs=[smem, smem],
        out_specs=[smem, smem],
        out_shape=[
            jax.ShapeDtypeStruct((SLOTS,), I32),
            jax.ShapeDtypeStruct((8, 128), I32),
        ],
        scratch_shapes=[pltpu.SMEM((SLOTS // 2,), I32)],
        name="tables",
    )(owner, agg_local)


def coarse_kernel(
    elem, near, slot, label, a_hbm, p_hbm, out,
    av, pv, sv, left, right, opp, relay, zs, zr, lv, names,
    in_sem, halo_send, halo_recv, lab_send, lab_recv, lab_sem, x_send, x_recv, z_send, z_recv,
):
    elems, blk, _ = p_hbm.shape
    part = blk // PIECES
    ng, nd = lax.axis_size("grp"), lax.axis_size("dev")
    g = lax.axis_index("grp")
    d = lax.axis_index("dev")
    z = d // NX
    x = d % NX
    xr = (g, z * NX + (x + 1) % NX)
    xl = (g, z * NX + (x + NX - 1) % NX)
    xo = (g, z * NX + (x + 2) % NX)
    zu = (g, ((z + 1) % NZ) * NX + x)
    zd = (g, ((z + NZ - 1) % NZ) * NX + x)

    halos = (
        (d < nd - 1, (g, (d + 1) % nd), d > 0),
        (d > 0, (g, (d + nd - 1) % nd), d < nd - 1),
        (g < ng - 1, ((g + 1) % ng, d), g > 0),
        (g > 0, ((g + ng - 1) % ng, d), g < ng - 1),
    )

    load_p = pltpu.make_async_copy(p_hbm, pv.at[0], in_sem.at[0])
    load_a = pltpu.make_async_copy(a_hbm, av, in_sem.at[1])
    load_p.start()
    load_a.start()

    barrier = pltpu.get_barrier_semaphore()
    expected = 5
    for peer in (xr, xl, xo, zu, zd):
        pl.semaphore_signal(barrier, inc=1, device_id=peer, device_id_type=MESH)
    for sends, peer, gets in halos:
        @pl.when(sends)
        def _():
            pl.semaphore_signal(barrier, inc=1, device_id=peer, device_id_type=MESH)

        expected = expected + jnp.where(gets, 1, 0)
    pl.semaphore_wait(barrier, expected)

    def halo_copy(i):
        return pltpu.make_async_remote_copy(
            src_ref=p_hbm,
            dst_ref=pv.at[1 + i],
            send_sem=halo_send.at[i],
            recv_sem=halo_recv.at[i],
            device_id=halos[i][1],
            device_id_type=MESH,
        )

    for i in range(4):
        @pl.when(halos[i][0])
        def _():
            halo_copy(i).start()

    def label_copy(i):
        return pltpu.make_async_remote_copy(
            src_ref=label,
            dst_ref=lv.at[1 + i],
            send_sem=lab_send.at[i],
            recv_sem=lab_recv.at[i],
            device_id=(xr, xl, xo)[i],
            device_id_type=MESH,
        )

    for i in range(3):
        label_copy(i).start()
    lv[0] = label[...]

    for i in range(4):
        @pl.when(jnp.logical_not(halos[i][2]))
        def _():
            def clear(e, carry):
                pv[1 + i, e] = jnp.zeros((blk, blk), BF)
                return carry

            lax.fori_loop(0, elems, clear, 0)

    for i in range(3):
        label_copy(i).wait_recv()
    load_names = pltpu.make_async_copy(lv, names, lab_sem.at[0])
    load_names.start()
    load_p.wait()
    load_a.wait()
    for i in (2, 3, 0, 1):
        @pl.when(halos[i][2])
        def _():
            halo_copy(i).wait_recv()

    def base(t, dx):
        return 2 * (((z + RELS[t]) % NZ) * NX + (x + dx) % NX)

    def compute(t, dx):
        for k in range(2):
            e = elem[base(t, dx) + k]
            own = pv[0, e]
            weighted = []
            for f in range(KC):
                face = own if f == 0 else pv[SOURCE[f], near[f - 1, e]]
                applied = jnp.dot(av[e, f], face, preferred_element_type=F32).astype(BF)
                weighted.append(
                    lax.dot_general(
                        own, applied, (((0,), (0,)), ((), ())), preferred_element_type=F32
                    )
                )
            for s in range(KC):
                total = None
                for f in range(KC):
                    term = jnp.where(slot[f, e] == s, weighted[f], 0.0)
                    total = term if total is None else total + term
                sv[(t % RING) * 8 + 2 * dx + k, s] = total.astype(BF)

    def compute_all(t):
        def one(dx, carry):
            compute(t, dx)
            return carry

        lax.fori_loop(0, NX, one, 0)

    def rows_of(p):
        return pl.ds(p * part, part)

    def remote(kind, t, p, src, dst, peer):
        n = t * PIECES + p
        return pltpu.make_async_remote_copy(
            src_ref=src,
            dst_ref=dst,
            send_sem=x_send.at[kind, n],
            recv_sem=x_recv.at[kind, n],
            device_id=peer,
            device_id_type=MESH,
        )

    def first_hop(t, p):
        r = rows_of(p)
        two = pl.ds(2 * t, 2)
        q = (t % RING) * 8
        return (
            remote(0, t, p, sv.at[q + 4, :, r], relay.at[2 * t, :, r], xr),
            remote(1, t, p, sv.at[q + 5, :, r], relay.at[2 * t + 1, :, r], xl),
            remote(2, t, p, sv.at[pl.ds(q + 2, 2), :, r], left.at[two, :, r], xr),
            remote(3, t, p, sv.at[pl.ds(q + 6, 2), :, r], right.at[two, :, r], xl),
        )

    def second_hop(t, p):
        r = rows_of(p)
        return (
            remote(4, t, p, relay.at[2 * t, :, r], opp.at[2 * t, :, r], xr),
            remote(5, t, p, relay.at[2 * t + 1, :, r], opp.at[2 * t + 1, :, r], xl),
        )

    def z_copy(way, k, p):
        n = (way * 4 + k - 1) * PIECES + p
        count = 4 if k == 4 else AGG
        return pltpu.make_async_remote_copy(
            src_ref=zs.at[way, pl.ds(ZOUT[k], count), :, rows_of(p)],
            dst_ref=zr.at[way, pl.ds(ZIN[k], count), :, rows_of(p)],
            send_sem=z_send.at[n],
            recv_sem=z_recv.at[n],
            device_id=zu if way == 0 else zd,
            device_id_type=MESH,
        )

    def combine(t, p, first, count, arrived, put):
        r = rows_of(p)
        own_of = [names[src, 0, base(t, 0) + k] for src in range(4) for k in range(2)]
        rows = [(sv, (t % RING) * 8), (left, 2 * t), (right, 2 * t), (opp, 2 * t)]

        def one(i, carry):
            a = first + i
            picks = [name == a for name in own_of]

            def block(s, inner):
                total = None
                for ref in arrived:
                    term = ref(i, s).astype(F32)
                    total = term if total is None else total + term
                n = 0
                for ref, q in rows:
                    for k in range(2):
                        term = jnp.where(picks[n], ref[q + k, s, r].astype(F32), 0.0)
                        total = term if total is None else total + term
                        n += 1
                put(i, s, total.astype(BF))
                return inner

            return lax.fori_loop(0, KC, block, carry)

        lax.fori_loop(0, count, one, 0)

    def from_z(way, row, p):
        return lambda i, s: zr[way, row + i, s, rows_of(p)]

    def to_z(way, row, p):
        def put(i, s, value):
            zs[way, row + i, s, rows_of(p)] = value

        return put

    def step(t, p):
        rel = RELS[t]
        if rel == 4:
            for way in range(2):
                combine(t, p, 4 * way, 4, (), to_z(way, ZOUT[4], p))
                z_copy(way, 4, p).start()
        elif rel == 0:
            for way in range(2):
                z_copy(way, 1, p).wait_recv()

            def put(i, s, value):
                out[i, s, rows_of(p)] = value

            combine(t, p, 0, AGG, (from_z(0, ZIN[1], p), from_z(1, ZIN[1], p)), put)
        else:
            way, k = (0, rel) if rel < 4 else (1, NZ - rel)
            if k == 1:
                z_copy(way, 3, p).wait_send()
            z_copy(way, k + 1, p).wait_recv()
            if k == 3:
                for half in range(2):
                    arrived = (from_z(way, ZIN[4], p),) if half == way else ()
                    combine(t, p, 4 * half, 4, arrived, to_z(way, ZOUT[3] + 4 * half, p))
            else:
                combine(t, p, 0, AGG, (from_z(way, ZIN[k + 1], p),), to_z(way, ZOUT[k], p))
            z_copy(way, k, p).start()

    start_t, start_p = ORDER[0]
    hop = first_hop(start_t, start_p)
    compute(start_t, 2)
    hop[0].start()
    hop[1].start()
    compute(start_t, 1)
    hop[2].start()
    compute(start_t, 3)
    hop[3].start()
    compute(start_t, 0)
    load_names.wait()
    done = {start_t}
    for n, (t, p) in enumerate(ORDER):
        hop = first_hop(t, p)
        again = second_hop(t, p)
        for way in range(2):
            hop[way].wait_recv()
            again[way].start()
        if n + 1 < len(ORDER):
            for copy in first_hop(*ORDER[n + 1]):
                copy.start()
        if n + 2 < len(ORDER) and ORDER[n + 2][0] not in done:
            later = ORDER[n + 2][0]
            done.add(later)
            if later >= RING:
                for q in range(PIECES):
                    for copy in first_hop(later - RING, q):
                        copy.wait_send()
            compute_all(later)
        hop[2].wait_recv()
        hop[3].wait_recv()
        again[0].wait_recv()
        again[1].wait_recv()
        step(t, p)
    for t, p in ORDER:
        copies = second_hop(t, p)
        if t + RING >= NZ:
            copies = copies + first_hop(t, p)
        for copy in copies:
            copy.wait_send()
    for way in range(2):
        for k in (1, 2, 4):
            for p in range(PIECES):
                z_copy(way, k, p).wait_send()
    for i in range(3):
        label_copy(i).wait_send()
    for i in range(4):
        @pl.when(halos[i][0])
        def _():
            halo_copy(i).wait_send()


def make_coarse(elem, near, slot, label, a_blocks, p_blocks):
    elems, blk, _ = p_blocks.shape
    block = (KC, blk, blk)
    n = NZ * PIECES
    smem = pl.BlockSpec(memory_space=pltpu.SMEM)
    hbm = pl.BlockSpec(memory_space=pl.ANY)
    dma = pltpu.SemaphoreType.DMA
    return pl.pallas_call(
        coarse_kernel,
        in_specs=[smem, smem, smem, pl.BlockSpec(memory_space=pltpu.VMEM), hbm, hbm],
        out_specs=pl.BlockSpec(memory_space=pltpu.VMEM),
        out_shape=jax.ShapeDtypeStruct((AGG,) + block, BF),
        scratch_shapes=[
            pltpu.VMEM((elems,) + block, BF),
            pltpu.VMEM((5, elems, blk, blk), BF),
            pltpu.VMEM((8 * RING,) + block, BF),
            pltpu.VMEM((2 * NZ,) + block, BF),
            pltpu.VMEM((2 * NZ,) + block, BF),
            pltpu.VMEM((2 * NZ,) + block, BF),
            pltpu.VMEM((2 * NZ,) + block, BF),
            pltpu.VMEM((2, ZOUT_ROWS) + block, BF),
            pltpu.VMEM((2, ZIN_ROWS) + block, BF),
            pltpu.VMEM((4, 8, 128), I32),
            pltpu.SMEM((4, 8, 128), I32),
            dma((2,)),
            dma((4,)),
            dma((4,)),
            dma((3,)),
            dma((3,)),
            dma((1,)),
            dma((6, n)),
            dma((6, n)),
            dma((n,)),
            dma((n,)),
        ],
        compiler_params=pltpu.CompilerParams(
            collective_id=0, has_side_effects=True, vmem_limit_bytes=63 << 20
        ),
        name="coarse",
    )(elem, near, slot, label, a_blocks, p_blocks)


def on_device(a_blocks, p_blocks, neighbours, coarse_slot, owner, agg_local):
    elem, label = make_tables(owner.T, agg_local[None, :])
    return make_coarse(elem, neighbours.T, coarse_slot.T, label, a_blocks, p_blocks)


def solution(mesh):
    placed = (
        P(("grp", "dev"), None, None, None),
        P(("grp", "dev"), None, None),
        P(("grp", "dev"), None),
        P(("grp", "dev"), None),
        P(("grp", "dev"), None),
        P(("grp", "dev")),
    )
    return jax.shard_map(
        on_device,
        mesh=mesh,
        in_specs=placed,
        out_specs=P(("grp", "dev"), None, None, None),
        check_vma=False,
    )
```

time: 237 us -> 206 us (0.87)
  starting transfers between devices: 18.7 us -> 0 us
  waiting for transfers between devices: 17.9 us -> 0 us
  Pallas kernels: 187 us -> 203 us
  local copies, waits for them, and re-layouts: 9.01 us -> 2.94 us
  other arithmetic: 2.97 us -> 0 us
    ppermute x7 -> x0, starting transfers between devices: 18.7 us -> none  [the longest x4 13 us: halo(): return lax.ppermute(p_blocks, axis, perm)]
    ppermute x7 -> x0, waiting for transfers between devices: 17.9 us -> none  [the longest x3 17.9 us: from_x(): return lax.ppermute(labels, 'dev', perm)]
    pallas_call x2, Pallas kernels: 187 us -> 203 us  [the longest x1 200 us: make_coarse(): pl.pallas_call(coarse_kernel, in_specs=[smem, smem, smem, pl.BlockSpec(me...]
    unnamed x7 -> x1, local copies, waits for them, and re-layouts: 8.81 us -> 2.94 us
  transfers between devices with their start and end apart: 7 -> 0, of which waited for: 2 -> 0; matrix products, arithmetic and copies ran while one was open for 2% -> 0% of each run, Pallas kernels for 0% -> 0%
where the time goes in v2:
time: 206 us
  Pallas kernels  203 us (99%)
  local copies, waits for them, and re-layouts  2.94 us (1%)
    pallas_call x1, Pallas kernels, make_coarse(): pl.pallas_call(coarse_kernel, in_specs=[smem, smem, smem, pl.BlockSpec(me...  200 us

profile of v2, /device:TPU:22, one launch (start us, length us, event | category | flops | bytes accessed | tf_op | source)
XLA Modules:
  0.0 205.6 jit_solution(6847798384901617846)
XLA Ops:
  0.0 2.3 %tables.1 = (s32[64]{0:T(128)}, s32[8,128]{1,0:T(8,128)}) custom-call(s32[1,32]{1,0:T(1,128)} %bitcast.6, s32[1,32]{1,0:T(1,128)} %bitcast.7), custom_call_target="tpu_custom_call" | custom-call | tf_op jit(solution)/shard_map/tables/pallas_call | solution.py:59
  2.4 200.3 %coarse.1 = bf16[8,7,128,128]{3,2,1,0:T(8,128)(2,1)} custom-call(s32[64]{0:T(128)} %get-tuple-element.7.elem, s32[6,32]{1,0:T(8,128)} %bitcast.4, s32[7,32]{1,0:T(8,128)} %bitcast.5, s32[8,128]{1,0:T(8,128)} %get-tuple-element.8.label, bf16[32,7,128,128]{3,2,1,0:T(8,128)(2,1)} %a_hbm.1, bf16[32,128,128]{2,1,0:T(8,128)(2,1)} %p_hbm.1), custom_call_target="tpu_custom_call" | custom-call | tf_op jit(solution)/shard_map/coarse/pallas_call | solution.py:359
  202.7 2.9 %copy.8 = bf16[8,7,128,128]{3,2,1,0:T(8,128)(2,1)} copy(bf16[8,7,128,128]{3,2,1,0:T(8,128)(2,1)} %coarse.1) | data formatting | bytes 3670016

commit v3 on v2

--- a/solution.py
+++ b/solution.py
@@ -31,48 +31,10 @@
 SOURCE = (0, 0, 0, 1, 2, 3, 4)
 
 
-def tables_kernel(owner, agg_local, elem, label, used):
-    def clear(i, carry):
-        elem[i] = 0
-        label[0, i] = -1
-        return carry
-
-    def clear_used(i, carry):
-        used[i] = 0
-        return carry
-
-    def place(e, carry):
-        o = owner[0, e]
-        r = 2 * o + used[o]
-        used[o] = used[o] + 1
-        elem[r] = e
-        label[0, r] = agg_local[0, e]
-        return carry
-
-    lax.fori_loop(0, SLOTS, clear, 0)
-    lax.fori_loop(0, SLOTS // 2, clear_used, 0)
-    lax.fori_loop(0, owner.shape[1], place, 0)
-
-
-def make_tables(owner, agg_local):
-    smem = pl.BlockSpec(memory_space=pltpu.SMEM)
-    return pl.pallas_call(
-        tables_kernel,
-        in_specs=[smem, smem],
-        out_specs=[smem, smem],
-        out_shape=[
-            jax.ShapeDtypeStruct((SLOTS,), I32),
-            jax.ShapeDtypeStruct((8, 128), I32),
-        ],
-        scratch_shapes=[pltpu.SMEM((SLOTS // 2,), I32)],
-        name="tables",
-    )(owner, agg_local)
-
-
 def coarse_kernel(
-    elem, near, slot, label, a_hbm, p_hbm, out,
-    av, pv, sv, left, right, opp, relay, zs, zr, lv, names,
-    in_sem, halo_send, halo_recv, lab_send, lab_recv, lab_sem, x_send, x_recv, z_send, z_recv,
+    owner, agg_local, near, slot, a_hbm, p_hbm, out,
+    av, pv, sv, left, right, opp, relay, zs, zr, result, lv, names, elem, twin, label,
+    in_sem, out_sem, halo_send, halo_recv, lab_send, lab_recv, lab_sem, x_send, x_recv, z_send, z_recv,
 ):
     elems, blk, _ = p_hbm.shape
     part = blk // PIECES
@@ -84,8 +46,9 @@
     xr = (g, z * NX + (x + 1) % NX)
     xl = (g, z * NX + (x + NX - 1) % NX)
     xo = (g, z * NX + (x + 2) % NX)
-    zu = (g, ((z + 1) % NZ) * NX + x)
-    zd = (g, ((z + NZ - 1) % NZ) * NX + x)
+    sense = 1 + (NZ - 2) * (g % 2)
+    zu = (g, ((z + sense) % NZ) * NX + x)
+    zd = (g, ((z + NZ - sense) % NZ) * NX + x)
 
     halos = (
         (d < nd - 1, (g, (d + 1) % nd), d > 0),
@@ -128,7 +91,7 @@
 
     def label_copy(i):
         return pltpu.make_async_remote_copy(
-            src_ref=label,
+            src_ref=lv.at[0],
             dst_ref=lv.at[1 + i],
             send_sem=lab_send.at[i],
             recv_sem=lab_recv.at[i],
@@ -136,9 +99,30 @@
             device_id_type=MESH,
         )
 
+    def place(o, carry):
+        one, two = -1, -1
+        for i in range(elems):
+            e = elems - 1 - i
+            here = owner[0, e] == o
+            two = jnp.where(here, one, two)
+            one = jnp.where(here, e, one)
+        first, second = jnp.maximum(one, 0), jnp.maximum(two, 0)
+        name = jnp.where(one < 0, -1, agg_local[0, first])
+        other = jnp.where(two < 0, -1, agg_local[0, second])
+        same = jnp.logical_and(two >= 0, name == other)
+        elem[2 * o] = first
+        elem[2 * o + 1] = second
+        twin[o] = jnp.where(same, 1, 0)
+        label[0, 2 * o] = name
+        label[0, 2 * o + 1] = jnp.where(same, -1, other)
+        return carry
+
+    lax.fori_loop(0, SLOTS // 2, place, 0)
+    share = pltpu.make_async_copy(label, lv.at[0], lab_sem.at[1])
+    share.start()
+    share.wait()
     for i in range(3):
         label_copy(i).start()
-    lv[0] = label[...]
 
     for i in range(4):
         @pl.when(jnp.logical_not(halos[i][2]))
@@ -161,10 +145,10 @@
             halo_copy(i).wait_recv()
 
     def base(t, dx):
-        return 2 * (((z + RELS[t]) % NZ) * NX + (x + dx) % NX)
+        return 2 * (((z + sense * RELS[t]) % NZ) * NX + (x + dx) % NX)
 
     def compute(t, dx):
-        for k in range(2):
+        for k in (1, 0):
             e = elem[base(t, dx) + k]
             own = pv[0, e]
             weighted = []
@@ -181,7 +165,11 @@
                 for f in range(KC):
                     term = jnp.where(slot[f, e] == s, weighted[f], 0.0)
                     total = term if total is None else total + term
-                sv[(t % RING) * 8 + 2 * dx + k, s] = total.astype(BF)
+                row = (t % RING) * 8 + 2 * dx
+                if k == 0:
+                    second = sv[row + 1, s].astype(F32)
+                    total = total + jnp.where(twin[base(t, dx) // 2] == 1, second, 0.0)
+                sv[row + k, s] = total.astype(BF)
 
     def compute_all(t):
         def one(dx, carry):
@@ -248,12 +236,11 @@
                 for ref in arrived:
                     term = ref(i, s).astype(F32)
                     total = term if total is None else total + term
-                n = 0
-                for ref, q in rows:
-                    for k in range(2):
-                        term = jnp.where(picks[n], ref[q + k, s, r].astype(F32), 0.0)
-                        total = term if total is None else total + term
-                        n += 1
+                nothing = jnp.zeros((part, blk), BF)
+                for n, (ref, q) in enumerate(rows):
+                    term = lax.select(picks[2 * n + 1], ref[q + 1, s, r], nothing)
+                    term = lax.select(picks[2 * n], ref[q, s, r], term).astype(F32)
+                    total = term if total is None else total + term
                 put(i, s, total.astype(BF))
                 return inner
 
@@ -269,6 +256,11 @@
             zs[way, row + i, s, rows_of(p)] = value
 
         return put
+
+    def out_copy(p):
+        return pltpu.make_async_copy(
+            result.at[:, :, rows_of(p)], out.at[:, :, rows_of(p)], out_sem.at[p]
+        )
 
     def step(t, p):
         rel = RELS[t]
@@ -281,9 +273,10 @@
                 z_copy(way, 1, p).wait_recv()
 
             def put(i, s, value):
-                out[i, s, rows_of(p)] = value
+                result[i, s, rows_of(p)] = value
 
             combine(t, p, 0, AGG, (from_z(0, ZIN[1], p), from_z(1, ZIN[1], p)), put)
+            out_copy(p).start()
         else:
             way, k = (0, rel) if rel < 4 else (1, NZ - rel)
             if k == 1:
@@ -343,13 +336,15 @@
                 z_copy(way, k, p).wait_send()
     for i in range(3):
         label_copy(i).wait_send()
+    for p in range(PIECES):
+        out_copy(p).wait()
     for i in range(4):
         @pl.when(halos[i][0])
         def _():
             halo_copy(i).wait_send()
 
 
-def make_coarse(elem, near, slot, label, a_blocks, p_blocks):
+def make_coarse(owner, agg_local, near, slot, a_blocks, p_blocks):
     elems, blk, _ = p_blocks.shape
     block = (KC, blk, blk)
     n = NZ * PIECES
@@ -358,8 +353,8 @@
     dma = pltpu.SemaphoreType.DMA
     return pl.pallas_call(
         coarse_kernel,
-        in_specs=[smem, smem, smem, pl.BlockSpec(memory_space=pltpu.VMEM), hbm, hbm],
-        out_specs=pl.BlockSpec(memory_space=pltpu.VMEM),
+        in_specs=[smem, smem, smem, smem, hbm, hbm],
+        out_specs=hbm,
         out_shape=jax.ShapeDtypeStruct((AGG,) + block, BF),
         scratch_shapes=[
             pltpu.VMEM((elems,) + block, BF),
@@ -371,29 +366,35 @@
             pltpu.VMEM((2 * NZ,) + block, BF),
             pltpu.VMEM((2, ZOUT_ROWS) + block, BF),
             pltpu.VMEM((2, ZIN_ROWS) + block, BF),
+            pltpu.VMEM((AGG,) + block, BF),
             pltpu.VMEM((4, 8, 128), I32),
             pltpu.SMEM((4, 8, 128), I32),
+            pltpu.SMEM((SLOTS,), I32),
+            pltpu.SMEM((SLOTS // 2,), I32),
+            pltpu.SMEM((8, 128), I32),
             dma((2,)),
+            dma((PIECES,)),
             dma((4,)),
             dma((4,)),
             dma((3,)),
             dma((3,)),
-            dma((1,)),
+            dma((2,)),
             dma((6, n)),
             dma((6, n)),
             dma((n,)),
             dma((n,)),
         ],
         compiler_params=pltpu.CompilerParams(
-            collective_id=0, has_side_effects=True, vmem_limit_bytes=63 << 20
+            collective_id=0, has_side_effects=True, vmem_limit_bytes=60 << 20
         ),
         name="coarse",
-    )(elem, near, slot, label, a_blocks, p_blocks)
+    )(owner, agg_local, near, slot, a_blocks, p_blocks)
 
 
 def on_device(a_blocks, p_blocks, neighbours, coarse_slot, owner, agg_local):
-    elem, label = make_tables(owner.T, agg_local[None, :])
-    return make_coarse(elem, neighbours.T, coarse_slot.T, label, a_blocks, p_blocks)
+    return make_coarse(
+        owner.T, agg_local[None, :], neighbours.T, coarse_slot.T, a_blocks, p_blocks
+    )
 
 
 def solution(mesh):

time: 206 us -> 200 us (0.971)
  Pallas kernels: 203 us -> 197 us
    pallas_call x2 -> x1, Pallas kernels: 203 us -> 197 us  [make_coarse(): pl.pallas_call(coarse_kernel, in_specs=[smem, smem, smem, smem, hbm, hbm]...]
where the time goes in v3:
time: 200 us; the launch traced here: 199 us
  Pallas kernels  197 us (98%)
  local copies, waits for them, and re-layouts  2.94 us (1%)
    pallas_call x1, Pallas kernels, make_coarse(): pl.pallas_call(coarse_kernel, in_specs=[smem, smem, smem, smem, hbm, hbm]...  197 us

profile of v3, /device:TPU:22, one launch (start us, length us, event | category | flops | bytes accessed | tf_op | source)
XLA Modules:
  0.0 199.5 jit_solution(10688390084756566175)
XLA Ops:
  0.0 196.5 %coarse.1 = bf16[8,7,128,128]{3,2,1,0:T(8,128)(2,1)} custom-call(s32[1,32]{1,0:T(1,128)} %bitcast.6, s32[1,32]{1,0:T(1,128)} %bitcast.7, s32[6,32]{1,0:T(8,128)} %bitcast.4, s32[7,32]{1,0:T(8,128)} %bitcast.5, bf16[32,7,128,128]{3,2,1,0:T(8,128)(2,1)} %a_hbm.1, bf16[32,128,128]{2,1,0:T(8,128)(2,1)} %p_hbm.1), custom_call_target="tpu_custom_call" | custom-call | tf_op jit(solution)/shard_map/coarse/pallas_call | solution.py:354
  196.5 2.9 %copy.8 = bf16[8,7,128,128]{3,2,1,0:T(8,128)(2,1)} copy(bf16[8,7,128,128]{3,2,1,0:T(8,128)(2,1)} %coarse.1) | data formatting | bytes 3670016

commit v4 on v3

--- a/solution.py
+++ b/solution.py
@@ -10,7 +10,8 @@
 NZ = 8
 AGG = 8
 SLOTS = 2 * NX * NZ
-PIECES = 2
+SPLIT = ((0, 4), (4, 3))
+PIECES = len(SPLIT)
 RING = 4
 MESH = pl.DeviceIdType.MESH
 BF = jnp.bfloat16
@@ -33,11 +34,10 @@
 
 def coarse_kernel(
     owner, agg_local, near, slot, a_hbm, p_hbm, out,
-    av, pv, sv, left, right, opp, relay, zs, zr, result, lv, names, elem, twin, label,
-    in_sem, out_sem, halo_send, halo_recv, lab_send, lab_recv, lab_sem, x_send, x_recv, z_send, z_recv,
+    av, pv, sv, left, right, opp, relay, zs, zr, lv, names, elem, twin, label,
+    in_sem, halo_send, halo_recv, lab_send, lab_recv, lab_sem, x_send, x_recv, z_send, z_recv,
 ):
     elems, blk, _ = p_hbm.shape
-    part = blk // PIECES
     ng, nd = lax.axis_size("grp"), lax.axis_size("dev")
     g = lax.axis_index("grp")
     d = lax.axis_index("dev")
@@ -147,8 +147,8 @@
     def base(t, dx):
         return 2 * (((z + sense * RELS[t]) % NZ) * NX + (x + dx) % NX)
 
-    def compute(t, dx):
-        for k in (1, 0):
+    def compute(t, dx, rows=(1, 0)):
+        for k in rows:
             e = elem[base(t, dx) + k]
             own = pv[0, e]
             weighted = []
@@ -178,8 +178,8 @@
 
         lax.fori_loop(0, NX, one, 0)
 
-    def rows_of(p):
-        return pl.ds(p * part, part)
+    def slots_of(p):
+        return pl.ds(*SPLIT[p])
 
     def remote(kind, t, p, src, dst, peer):
         n = t * PIECES + p
@@ -193,29 +193,29 @@
         )
 
     def first_hop(t, p):
-        r = rows_of(p)
+        r = slots_of(p)
         two = pl.ds(2 * t, 2)
         q = (t % RING) * 8
         return (
-            remote(0, t, p, sv.at[q + 4, :, r], relay.at[2 * t, :, r], xr),
-            remote(1, t, p, sv.at[q + 5, :, r], relay.at[2 * t + 1, :, r], xl),
-            remote(2, t, p, sv.at[pl.ds(q + 2, 2), :, r], left.at[two, :, r], xr),
-            remote(3, t, p, sv.at[pl.ds(q + 6, 2), :, r], right.at[two, :, r], xl),
+            remote(0, t, p, sv.at[q + 4, r], relay.at[2 * t, r], xr),
+            remote(1, t, p, sv.at[q + 5, r], relay.at[2 * t + 1, r], xl),
+            remote(2, t, p, sv.at[pl.ds(q + 2, 2), r], left.at[two, r], xr),
+            remote(3, t, p, sv.at[pl.ds(q + 6, 2), r], right.at[two, r], xl),
         )
 
     def second_hop(t, p):
-        r = rows_of(p)
+        r = slots_of(p)
         return (
-            remote(4, t, p, relay.at[2 * t, :, r], opp.at[2 * t, :, r], xr),
-            remote(5, t, p, relay.at[2 * t + 1, :, r], opp.at[2 * t + 1, :, r], xl),
+            remote(4, t, p, relay.at[2 * t, r], opp.at[2 * t, r], xr),
+            remote(5, t, p, relay.at[2 * t + 1, r], opp.at[2 * t + 1, r], xl),
         )
 
     def z_copy(way, k, p):
         n = (way * 4 + k - 1) * PIECES + p
         count = 4 if k == 4 else AGG
         return pltpu.make_async_remote_copy(
-            src_ref=zs.at[way, pl.ds(ZOUT[k], count), :, rows_of(p)],
-            dst_ref=zr.at[way, pl.ds(ZIN[k], count), :, rows_of(p)],
+            src_ref=zs.at[way, pl.ds(ZOUT[k], count), slots_of(p)],
+            dst_ref=zr.at[way, pl.ds(ZIN[k], count), slots_of(p)],
             send_sem=z_send.at[n],
             recv_sem=z_recv.at[n],
             device_id=zu if way == 0 else zd,
@@ -223,7 +223,7 @@
         )
 
     def combine(t, p, first, count, arrived, put):
-        r = rows_of(p)
+        low, slots = SPLIT[p]
         own_of = [names[src, 0, base(t, 0) + k] for src in range(4) for k in range(2)]
         rows = [(sv, (t % RING) * 8), (left, 2 * t), (right, 2 * t), (opp, 2 * t)]
 
@@ -231,36 +231,32 @@
             a = first + i
             picks = [name == a for name in own_of]
 
-            def block(s, inner):
+            def block(n, inner):
+                s = low + n
                 total = None
                 for ref in arrived:
                     term = ref(i, s).astype(F32)
                     total = term if total is None else total + term
-                nothing = jnp.zeros((part, blk), BF)
-                for n, (ref, q) in enumerate(rows):
-                    term = lax.select(picks[2 * n + 1], ref[q + 1, s, r], nothing)
-                    term = lax.select(picks[2 * n], ref[q, s, r], term).astype(F32)
+                nothing = jnp.zeros((blk, blk), BF)
+                for m, (ref, q) in enumerate(rows):
+                    term = lax.select(picks[2 * m + 1], ref[q + 1, s], nothing)
+                    term = lax.select(picks[2 * m], ref[q, s], term).astype(F32)
                     total = term if total is None else total + term
                 put(i, s, total.astype(BF))
                 return inner
 
-            return lax.fori_loop(0, KC, block, carry)
+            return lax.fori_loop(0, slots, block, carry)
 
         lax.fori_loop(0, count, one, 0)
 
     def from_z(way, row, p):
-        return lambda i, s: zr[way, row + i, s, rows_of(p)]
+        return lambda i, s: zr[way, row + i, s]
 
     def to_z(way, row, p):
         def put(i, s, value):
-            zs[way, row + i, s, rows_of(p)] = value
+            zs[way, row + i, s] = value
 
         return put
-
-    def out_copy(p):
-        return pltpu.make_async_copy(
-            result.at[:, :, rows_of(p)], out.at[:, :, rows_of(p)], out_sem.at[p]
-        )
 
     def step(t, p):
         rel = RELS[t]
@@ -273,10 +269,9 @@
                 z_copy(way, 1, p).wait_recv()
 
             def put(i, s, value):
-                result[i, s, rows_of(p)] = value
+                out[i, s] = value
 
             combine(t, p, 0, AGG, (from_z(0, ZIN[1], p), from_z(1, ZIN[1], p)), put)
-            out_copy(p).start()
         else:
             way, k = (0, rel) if rel < 4 else (1, NZ - rel)
             if k == 1:
@@ -292,9 +287,10 @@
 
     start_t, start_p = ORDER[0]
     hop = first_hop(start_t, start_p)
-    compute(start_t, 2)
+    compute(start_t, 2, (1,))
+    hop[1].start()
+    compute(start_t, 2, (0,))
     hop[0].start()
-    hop[1].start()
     compute(start_t, 1)
     hop[2].start()
     compute(start_t, 3)
@@ -336,8 +332,6 @@
                 z_copy(way, k, p).wait_send()
     for i in range(3):
         label_copy(i).wait_send()
-    for p in range(PIECES):
-        out_copy(p).wait()
     for i in range(4):
         @pl.when(halos[i][0])
         def _():
@@ -354,8 +348,8 @@
     return pl.pallas_call(
         coarse_kernel,
         in_specs=[smem, smem, smem, smem, hbm, hbm],
-        out_specs=hbm,
-        out_shape=jax.ShapeDtypeStruct((AGG,) + block, BF),
+        out_specs=pl.BlockSpec(memory_space=pltpu.VMEM),
+        out_shape=pltpu.VMEM((AGG,) + block, BF),
         scratch_shapes=[
             pltpu.VMEM((elems,) + block, BF),
             pltpu.VMEM((5, elems, blk, blk), BF),
@@ -366,14 +360,12 @@
             pltpu.VMEM((2 * NZ,) + block, BF),
             pltpu.VMEM((2, ZOUT_ROWS) + block, BF),
             pltpu.VMEM((2, ZIN_ROWS) + block, BF),
-            pltpu.VMEM((AGG,) + block, BF),
             pltpu.VMEM((4, 8, 128), I32),
             pltpu.SMEM((4, 8, 128), I32),
             pltpu.SMEM((SLOTS,), I32),
             pltpu.SMEM((SLOTS // 2,), I32),
             pltpu.SMEM((8, 128), I32),
             dma((2,)),
-            dma((PIECES,)),
             dma((4,)),
             dma((4,)),
             dma((3,)),

time: 200 us -> 197 us (0.985)
  Pallas kernels: 197 us -> 195 us
where the time goes in v4:
time: 197 us; the launch traced here: 196 us
  Pallas kernels  195 us (99%)
    pallas_call x1, Pallas kernels, make_coarse(): pl.pallas_call(coarse_kernel, in_specs=[smem, smem, smem, smem, hbm, hbm]...  195 us

profile of v4, /device:TPU:22, one launch (start us, length us, event | category | flops | bytes accessed | tf_op | source)
XLA Modules:
  0.0 196.2 jit_solution(15200636419452759541)
XLA Ops:
  0.0 195.0 %coarse.1 = bf16[8,7,128,128]{3,2,1,0:T(8,128)(2,1)S(1)} custom-call(s32[1,32]{1,0:T(1,128)} %bitcast.6, s32[1,32]{1,0:T(1,128)} %bitcast.7, s32[6,32]{1,0:T(8,128)} %bitcast.4, s32[7,32]{1,0:T(8,128)} %bitcast.5, bf16[32,7,128,128]{3,2,1,0:T(8,128)(2,1)} %a_hbm.1, bf16[32,128,128]{2,1,0:T(8,128)(2,1)} %p_hbm.1), custom_call_target="tpu_custom_call" | custom-call | tf_op jit(solution)/shard_map/coarse/pallas_call | solution.py:348
  195.0 1.2 copy.8

commit v5 on v4

--- a/solution.py
+++ b/solution.py
@@ -13,6 +13,7 @@
 SPLIT = ((0, 4), (4, 3))
 PIECES = len(SPLIT)
 RING = 4
+AHEAD = 2
 MESH = pl.DeviceIdType.MESH
 BF = jnp.bfloat16
 F32 = jnp.float32
@@ -33,9 +34,10 @@
 
 
 def coarse_kernel(
-    owner, agg_local, near, slot, a_hbm, p_hbm, out,
-    av, pv, sv, left, right, opp, relay, zs, zr, lv, names, elem, twin, label,
-    in_sem, halo_send, halo_recv, lab_send, lab_recv, lab_sem, x_send, x_recv, z_send, z_recv,
+    owner_hbm, agg_hbm, near_hbm, slot_hbm, a_hbm, p_hbm, out,
+    av, pv, sv, left, right, opp, zs, zr, lv, names, elem, twin, label,
+    owner, agg_local, near, slot,
+    in_sem, index_sem, halo_send, halo_recv, lab_send, lab_recv, lab_sem, x_send, x_recv, z_send, z_recv,
 ):
     elems, blk, _ = p_hbm.shape
     ng, nd = lax.axis_size("grp"), lax.axis_size("dev")
@@ -59,6 +61,14 @@
 
     load_p = pltpu.make_async_copy(p_hbm, pv.at[0], in_sem.at[0])
     load_a = pltpu.make_async_copy(a_hbm, av, in_sem.at[1])
+    indices = tuple(
+        pltpu.make_async_copy(source, target, index_sem.at[i])
+        for i, (source, target) in enumerate(
+            ((owner_hbm, owner), (agg_hbm, agg_local), (near_hbm, near), (slot_hbm, slot))
+        )
+    )
+    for copy in indices:
+        copy.start()
     load_p.start()
     load_a.start()
 
@@ -66,8 +76,8 @@
     expected = 5
     for peer in (xr, xl, xo, zu, zd):
         pl.semaphore_signal(barrier, inc=1, device_id=peer, device_id_type=MESH)
-    for sends, peer, gets in halos:
-        @pl.when(sends)
+    for has_receiver, peer, gets in halos:
+        @pl.when(has_receiver)
         def _():
             pl.semaphore_signal(barrier, inc=1, device_id=peer, device_id_type=MESH)
 
@@ -117,6 +127,8 @@
         label[0, 2 * o + 1] = jnp.where(same, -1, other)
         return carry
 
+    for copy in indices:
+        copy.wait()
     lax.fori_loop(0, SLOTS // 2, place, 0)
     share = pltpu.make_async_copy(label, lv.at[0], lab_sem.at[1])
     share.start()
@@ -147,8 +159,8 @@
     def base(t, dx):
         return 2 * (((z + sense * RELS[t]) % NZ) * NX + (x + dx) % NX)
 
-    def compute(t, dx, rows=(1, 0)):
-        for k in rows:
+    def compute(t, dx):
+        for k in (1, 0):
             e = elem[base(t, dx) + k]
             own = pv[0, e]
             weighted = []
@@ -192,22 +204,14 @@
             device_id_type=MESH,
         )
 
-    def first_hop(t, p):
+    def sends(t, p):
         r = slots_of(p)
         two = pl.ds(2 * t, 2)
         q = (t % RING) * 8
         return (
-            remote(0, t, p, sv.at[q + 4, r], relay.at[2 * t, r], xr),
-            remote(1, t, p, sv.at[q + 5, r], relay.at[2 * t + 1, r], xl),
-            remote(2, t, p, sv.at[pl.ds(q + 2, 2), r], left.at[two, r], xr),
-            remote(3, t, p, sv.at[pl.ds(q + 6, 2), r], right.at[two, r], xl),
-        )
-
-    def second_hop(t, p):
-        r = slots_of(p)
-        return (
-            remote(4, t, p, relay.at[2 * t, r], opp.at[2 * t, r], xr),
-            remote(5, t, p, relay.at[2 * t + 1, r], opp.at[2 * t + 1, r], xl),
+            remote(0, t, p, sv.at[pl.ds(q + 4, 2), r], opp.at[two, r], xo),
+            remote(1, t, p, sv.at[pl.ds(q + 2, 2), r], left.at[two, r], xr),
+            remote(2, t, p, sv.at[pl.ds(q + 6, 2), r], right.at[two, r], xl),
         )
 
     def z_copy(way, k, p):
@@ -285,47 +289,45 @@
                 combine(t, p, 0, AGG, (from_z(way, ZIN[k + 1], p),), to_z(way, ZOUT[k], p))
             z_copy(way, k, p).start()
 
-    start_t, start_p = ORDER[0]
-    hop = first_hop(start_t, start_p)
-    compute(start_t, 2, (1,))
-    hop[1].start()
-    compute(start_t, 2, (0,))
-    hop[0].start()
-    compute(start_t, 1)
-    hop[2].start()
-    compute(start_t, 3)
-    hop[3].start()
+    def issue(n):
+        for copy in sends(*ORDER[n]):
+            copy.start()
+
+    done = set()
+
+    def prepare(n):
+        if n >= len(ORDER) or ORDER[n][0] in done:
+            return
+        t = ORDER[n][0]
+        done.add(t)
+        if t >= RING:
+            for p in range(PIECES):
+                for copy in sends(t - RING, p):
+                    copy.wait_send()
+        compute_all(t)
+
+    start_t = ORDER[0][0]
+    done.add(start_t)
+    for dx, copy in zip((2, 1, 3), sends(*ORDER[0])):
+        compute(start_t, dx)
+        copy.start()
     compute(start_t, 0)
+    for n in range(1, AHEAD):
+        prepare(n)
+        issue(n)
+    prepare(AHEAD)
     load_names.wait()
-    done = {start_t}
     for n, (t, p) in enumerate(ORDER):
-        hop = first_hop(t, p)
-        again = second_hop(t, p)
-        for way in range(2):
-            hop[way].wait_recv()
-            again[way].start()
-        if n + 1 < len(ORDER):
-            for copy in first_hop(*ORDER[n + 1]):
-                copy.start()
-        if n + 2 < len(ORDER) and ORDER[n + 2][0] not in done:
-            later = ORDER[n + 2][0]
-            done.add(later)
-            if later >= RING:
-                for q in range(PIECES):
-                    for copy in first_hop(later - RING, q):
-                        copy.wait_send()
-            compute_all(later)
-        hop[2].wait_recv()
-        hop[3].wait_recv()
-        again[0].wait_recv()
-        again[1].wait_recv()
+        if n + AHEAD < len(ORDER):
+            issue(n + AHEAD)
+        prepare(n + AHEAD + 1)
+        for copy in sends(t, p):
+            copy.wait_recv()
         step(t, p)
     for t, p in ORDER:
-        copies = second_hop(t, p)
         if t + RING >= NZ:
-            copies = copies + first_hop(t, p)
-        for copy in copies:
-            copy.wait_send()
+            for copy in sends(t, p):
+                copy.wait_send()
     for way in range(2):
         for k in (1, 2, 4):
             for p in range(PIECES):
@@ -342,19 +344,17 @@
     elems, blk, _ = p_blocks.shape
     block = (KC, blk, blk)
     n = NZ * PIECES
-    smem = pl.BlockSpec(memory_space=pltpu.SMEM)
     hbm = pl.BlockSpec(memory_space=pl.ANY)
     dma = pltpu.SemaphoreType.DMA
     return pl.pallas_call(
         coarse_kernel,
-        in_specs=[smem, smem, smem, smem, hbm, hbm],
+        in_specs=[hbm] * 6,
         out_specs=pl.BlockSpec(memory_space=pltpu.VMEM),
         out_shape=pltpu.VMEM((AGG,) + block, BF),
         scratch_shapes=[
             pltpu.VMEM((elems,) + block, BF),
             pltpu.VMEM((5, elems, blk, blk), BF),
             pltpu.VMEM((8 * RING,) + block, BF),
-            pltpu.VMEM((2 * NZ,) + block, BF),
             pltpu.VMEM((2 * NZ,) + block, BF),
             pltpu.VMEM((2 * NZ,) + block, BF),
             pltpu.VMEM((2 * NZ,) + block, BF),
@@ -365,14 +365,19 @@
             pltpu.SMEM((SLOTS,), I32),
             pltpu.SMEM((SLOTS // 2,), I32),
             pltpu.SMEM((8, 128), I32),
+            pltpu.SMEM(owner.shape, I32),
+            pltpu.SMEM(agg_local.shape, I32),
+            pltpu.SMEM(near.shape, I32),
+            pltpu.SMEM(slot.shape, I32),
             dma((2,)),
+            dma((4,)),
             dma((4,)),
             dma((4,)),
             dma((3,)),
             dma((3,)),
             dma((2,)),
-            dma((6, n)),
-            dma((6, n)),
+            dma((3, n)),
+            dma((3, n)),
             dma((n,)),
             dma((n,)),
         ],

time: 197 us -> 196 us (level)
  Pallas kernels: 195 us -> 193 us
where the time goes in v5:
time: 196 us; the launch traced here: 194 us
  Pallas kernels  193 us (98%)
    pallas_call x1, Pallas kernels, make_coarse(): pl.pallas_call(coarse_kernel, in_specs=[hbm] * 6, out_specs=pl.BlockSpec(...  193 us

profile of v5, /device:TPU:22, one launch (start us, length us, event | category | flops | bytes accessed | tf_op | source)
XLA Modules:
  0.0 194.3 jit_solution(512052528301851508)
XLA Ops:
  0.0 193.0 %coarse.1 = bf16[8,7,128,128]{3,2,1,0:T(8,128)(2,1)S(1)} custom-call(s32[1,32]{1,0:T(1,128)} %bitcast.6, s32[1,32]{1,0:T(1,128)} %bitcast.7, s32[6,32]{1,0:T(8,128)} %bitcast.4, s32[7,32]{1,0:T(8,128)} %bitcast.5, bf16[32,7,128,128]{3,2,1,0:T(8,128)(2,1)} %a_hbm.1, bf16[32,128,128]{2,1,0:T(8,128)(2,1)} %p_hbm.1), custom_call_target="tpu_custom_call" | custom-call | tf_op jit(solution)/shard_map/coarse/pallas_call | solution.py:349
  193.0 1.2 copy.8

commit v6 on v5

--- a/solution.py
+++ b/solution.py
@@ -145,10 +145,6 @@
 
             lax.fori_loop(0, elems, clear, 0)
 
-    for i in range(3):
-        label_copy(i).wait_recv()
-    load_names = pltpu.make_async_copy(lv, names, lab_sem.at[0])
-    load_names.start()
     load_p.wait()
     load_a.wait()
     for i in (2, 3, 0, 1):
@@ -316,6 +312,10 @@
         prepare(n)
         issue(n)
     prepare(AHEAD)
+    for i in range(3):
+        label_copy(i).wait_recv()
+    load_names = pltpu.make_async_copy(lv, names, lab_sem.at[0])
+    load_names.start()
     load_names.wait()
     for n, (t, p) in enumerate(ORDER):
         if n + AHEAD < len(ORDER):

time: 196 us -> 196 us (level)
  no operation moved by 1% of the time
where the time goes in v6:
time: 196 us; the launch traced here: 194 us
  Pallas kernels  193 us (98%)
    pallas_call x1, Pallas kernels, make_coarse(): pl.pallas_call(coarse_kernel, in_specs=[hbm] * 6, out_specs=pl.BlockSpec(...  193 us

profile of v6, /device:TPU:22, one launch (start us, length us, event | category | flops | bytes accessed | tf_op | source)
XLA Modules:
  0.0 193.7 jit_solution(7137051001887679127)
XLA Ops:
  0.0 192.5 %coarse.1 = bf16[8,7,128,128]{3,2,1,0:T(8,128)(2,1)S(1)} custom-call(s32[1,32]{1,0:T(1,128)} %bitcast.6, s32[1,32]{1,0:T(1,128)} %bitcast.7, s32[6,32]{1,0:T(8,128)} %bitcast.4, s32[7,32]{1,0:T(8,128)} %bitcast.5, bf16[32,7,128,128]{3,2,1,0:T(8,128)(2,1)} %a_hbm.1, bf16[32,128,128]{2,1,0:T(8,128)(2,1)} %p_hbm.1), custom_call_target="tpu_custom_call" | custom-call | tf_op jit(solution)/shard_map/coarse/pallas_call | solution.py:349
  192.5 1.2 copy.8
